TPU v7x, 256 devices: a whole 4x4x8 slice. The times are simulated.
256 devices in a mesh: dp: 32 (over z_lo, x, core), seq: 8 (over z_hi, y).
Axes of the slice: x: 4, y: 4, z: 8 (z_hi: 2, z_lo: 4; z = z_hi * 4 + z_lo), core: 2. Of those that a mesh axis runs over, the one named last changes fastest.
Arguments:
- tokens: bfloat16 [32, 3072, 1024], P('dp', 'seq'), may hold values from -6 to 6
- masks: int32 [32, 24, 24], P('dp', 'seq'), may hold values from 0 to 1, as said below
- ln_gain: float32 [1024], replicated, may hold values from 0.25 to 1.75
- ln_bias: float32 [1024], replicated, may hold values from -3 to 3
- w_qkv: bfloat16 [1024, 3072], P('dp'), may hold values from -0.4 to 0.4
- qkv_bias: float32 [3072], replicated, may hold values from -3 to 3
- w_out: bfloat16 [1024, 1024], P('dp'), may hold values from -0.1875 to 0.1875
- out_bias: float32 [1024], replicated, may hold values from -2 to 2
Outputs:
- updated: bfloat16 [32, 3072, 1024], P('dp', 'seq')
- context: bfloat16 [32, 3072, 1024], P('dp', 'seq')
Inputs may be any that keep to these rules, and one draw needn't show every extreme that they name: Entries are 0 or 1; every diagonal entry masks[s, b, b] is 1.
All inputs are finite; a program needn't handle non-finite values.
Results may differ from a plain program's by a relative error of at most 0.012.
Values may be sent and summed in bfloat16 or wider, within the bound.
A program may use at most 192 MiB of HBM per device.

v0:
```python
import jax
import jax.numpy as jnp
from jax import lax
from jax.sharding import PartitionSpec as P

D = 1024
HEADS = 16
BLOCK = 128


NEG_FILL = -1e30
EPSILON = 1e-06


def from_behind(block, axis, distance):
    devices = range(lax.axis_size(axis))
    route = [((i - distance) % len(devices), i) for i in devices]
    return lax.ppermute(block, axis, route)


def layer_norm(sheet, ln_gain, ln_bias):
    values = sheet.astype(jnp.float32)
    center = jnp.mean(values, axis=-1, keepdims=True)
    spread = jnp.mean(jnp.square(values - center), axis=-1, keepdims=True)
    normed = (values - center) * lax.rsqrt(spread + EPSILON)
    return (normed * ln_gain + ln_bias).astype(jnp.bfloat16)


def row_adder(left_operand, shard_piece):
    return jnp.dot(left_operand, shard_piece, preferred_element_type=jnp.float32)


def attend(state_now, key_piece, value_piece, first_row, queries, mask_rows):
    key_rows = key_piece.shape[0]
    query_blocks = mask_rows.shape[0]
    head_dim = D // HEADS
    scaling = head_dim ** (-0.5)
    block_ids = (first_row + lax.iota(jnp.int32, key_rows)) // BLOCK
    picker = (block_ids[:, None] == lax.iota(jnp.int32, mask_rows.shape[1])[None, :]).astype(
        jnp.float32
    )
    tile_mask = jnp.dot(mask_rows.astype(jnp.float32), picker.T)
    allowed = jnp.broadcast_to(
        (tile_mask > 0.5)[:, None, :], (query_blocks, BLOCK, key_rows)
    ).reshape(query_blocks * BLOCK, key_rows)
    active = jnp.any(allowed)

    def update(inner):
        run_max, run_sum, weighted = inner
        token_count = weighted.shape[0]
        key_heads = key_piece.reshape(key_rows, HEADS, head_dim)
        value_heads = value_piece.reshape(key_rows, HEADS, head_dim)
        scores = (
            jnp.einsum("qhd,khd->hqk", queries, key_heads, preferred_element_type=jnp.float32)
            * scaling
        )
        masked = jnp.where(allowed[None], scores, NEG_FILL)
        new_max = jnp.maximum(run_max, jnp.max(masked, axis=2))
        weights = jnp.where(allowed[None], jnp.exp(scores - new_max[:, :, None]), 0.0)
        factor = jnp.exp(run_max - new_max)
        new_sum = run_sum * factor + jnp.sum(weights, axis=2)
        mixed = jnp.einsum(
            "hqk,khd->qhd",
            weights.astype(jnp.bfloat16),
            value_heads,
            preferred_element_type=jnp.float32,
        )
        rescaled = weighted.reshape(token_count, HEADS, head_dim) * factor.T[:, :, None]
        return (new_max, new_sum, (rescaled + mixed).reshape(token_count, HEADS * head_dim))

    def unchanged(inner):
        return inner

    return lax.cond(active, update, unchanged, state_now)


def on_device(tokens, masks, ln_gain, ln_bias, w_qkv, qkv_bias, w_out, out_bias):
    sheet = tokens[0]
    mask_rows = masks[0]
    tokens_here = sheet.shape[0]
    width = sheet.shape[1]
    head_dim = D // HEADS
    normed = layer_norm(sheet, ln_gain, ln_bias)
    packed_raw = row_adder(normed, lax.all_gather(w_qkv, "dp", axis=0, tiled=True))
    packed = (packed_raw + qkv_bias).astype(jnp.bfloat16)
    queries = packed[:, :width].reshape(tokens_here, HEADS, head_dim)
    key_part = packed[:, width : 2 * width]
    value_part = packed[:, 2 * width :]
    start_state = (
        jnp.full((HEADS, tokens_here), NEG_FILL, jnp.float32),
        jnp.zeros((HEADS, tokens_here), jnp.float32),
        jnp.zeros((tokens_here, width), jnp.float32),
    )
    position = lax.axis_index("seq")
    loop_size = lax.axis_size("seq")
    own_state = attend(
        start_state, key_part, value_part, position * tokens_here, queries, mask_rows
    )

    def hop_step(hop_index, loop_state):
        moving, inner = loop_state
        moving = from_behind(moving, "seq", 1)
        source = (position - hop_index) % loop_size
        inner = attend(inner, moving[0], moving[1], source * tokens_here, queries, mask_rows)
        return (moving, inner)

    moved_last, final_state = lax.fori_loop(
        1, loop_size, hop_step, (jnp.stack([key_part, value_part]), own_state)
    )
    run_max, run_sum, weighted = final_state
    context = (
        (weighted.reshape(tokens_here, HEADS, head_dim) / run_sum.T[:, :, None])
        .reshape(tokens_here, width)
        .astype(jnp.bfloat16)
    )
    projected = row_adder(context, lax.all_gather(w_out, "dp", axis=0, tiled=True))
    updated = (sheet.astype(jnp.float32) + projected + out_bias).astype(jnp.bfloat16)
    return (updated[None], context[None])


def solution(mesh):
    placed = (
        P("dp", "seq", None),
        P("dp", "seq", None),
        P(),
        P(),
        P("dp", None),
        P(),
        P("dp", None),
        P(),
    )
    return jax.shard_map(
        on_device,
        mesh=mesh,
        in_specs=placed,
        out_specs=(P("dp", "seq", None), P("dp", "seq", None)),
        check_vma=False,
    )
```

profile of v0, /device:TPU:28, one launch (start us, length us, event | category | flops | bytes accessed | tf_op | source)
XLA Modules:
  0.0 668.6 jit_solution(15713503643029758900)
XLA Ops:
  13.9 64.2 %all-gather.3.cloned.1.call-done = bf16[1024,3072]{1,0:T(8,128)(2,1)} async-done(((bf16[32,3072]{1,0:T(8,128)(2,1)}), bf16[1024,3072]{1,0:T(8,128)(2,1)}) %all-gather.3.cloned.1.call-update) | async-done | bytes 6291472 | tf_op jit(solution)/shard_map/all_gather | solution.py:84
  78.0 5.7 add_convert_fusion
  88.9 15.0 %conditional.2 = (f32[16,384]{1,0:T(8,128)}, f32[16,384]{1,0:T(8,128)S(1)}, f32[384,1024]{0,1:T(8,128)}) conditional(s32[]{:T(128)} %convert_element_type.61, () %tuple.45, (pred[3,128,384]{2,1,0:T(8,128)(4,1)S(1)}, bf16[384,1024]{1,0:T(8,128)(2,1)}, bf16[384,16,64]{0,2,1:T(8,128)(2,1)S(1)}, bf16[384,1024]{1,0:T(8,128)(2,1)S(1)}) %tuple.88), branch_computations={%region_3.4_spmd, %region_4.7_spmd} | conditional | flops 630349824 | bytes 74145848 | solution.py:74
  97.0 6.9 %bitcast_add_fusion = f32[384,16,64]{0,2,1:T(8,128)} fusion(bf16[384,16,64]{0,2,1:T(8,128)(2,1)S(1)} %bitcast.85, f32[16,384,384]{1,2,0:T(8,128)} %copy-done, f32[16,384]{1,0:T(8,128)} %get-tuple-element.392, pred[384,384]{0,1:T(8,128)(4,1)S(1)} %copy.21, f32[384,16]{0,1:T(8,128)S(1)} %get-tuple-element.313), kind=kOutput, calls=%fused_computation.6 | convolution fusion | flops 311820288 | bytes 11993088 | tf_op jit(solution)/shard_map/cond/branch_1_fun/hqk,khd->qhd/dot_general | solution.py:62
  103.9 551.5 %while.21 = (s32[]{:T(128)}, bf16[2,384,1024]{1,2,0:T(8,128)(2,1)}, f32[16,384]{1,0:T(8,128)}, f32[16,384]{1,0:T(8,128)S(1)}, f32[384,1024]{0,1:T(8,128)}, /*ind...) while((s32[]{:T(128)}, bf16[2,384,1024]{1,2,0:T(8,128)(2,1)}, ...), condition=%wide.region_13.14_spmd, body=%wide.region_7.13_spmd.sunk | while | flops 630956160 | bytes 47684524 | solution.py:107
  110.0 59.8 %collective-permute-done = bf16[2,384,1024]{1,2,0:T(8,128)(2,1)S(1)} collective-permute-done((bf16[2,384,1024]{1,2,0:T(8,128)(2,1)}, bf16[2,384,1024]{1,2,0:T(8,128)(2,1)S(1)}, u32[]{:S(2)}, u32[]{:S(2)}) %collective-permute-start) | collective-permute-done | bytes 1572896 | tf_op jit(solution)/shard_map/while/body/eval_jaxpr/ppermute | solution.py:18
  169.8 10.7 %conditional.4 = ((f32[16,384]{1,0:T(8,128)}, f32[16,384]{1,0:T(8,128)S(1)}, f32[384,1024]{0,1:T(8,128)})) conditional(s32[]{:T(128)} %convert_element_type.105, (f32[16,384]{1,0:T(8,128)}, f32[16,384]{1,0:T(8,128)S(1)}, f32[384,1024]{0,1:T(8,128)}) %tuple.73, (pred[3,128,384]{2,1,0:T(8,128)(4,1)S(1)}, bf16[2,384,1024]{1,2,0:T(8,128)(2,1)S(1)}, ...), branch_computations={%region_9.9_spmd, %region_10.12_spmd} | conditional | flops 630736896 | bytes 38092832 | solution.py:74
  175.3 4.6 bitcast_add_fusion.1
  181.7 15.6 %collective-permute-start = (bf16[2,384,1024]{1,2,0:T(8,128)(2,1)}, bf16[2,384,1024]{1,2,0:T(8,128)(2,1)S(1)}, u32[]{:S(2)}, u32[]{:S(2)}) collective-permute-start(bf16[2,384,1024]{1,2,0:T(8,128)(2,1)} %get-tuple-element.409), channel_id=1, source_target_pairs={{7,0},{0,1},{1,2},{2,3},{3,4},{4,5},{5,6},{6,7},{15,8},{8,9},{9,10... | collective-permute-start | bytes 4718600 | tf_op jit(solution)/shard_map/while/body/eval_jaxpr/ppermute | solution.py:18
  199.0 58.8 %collective-permute-done = bf16[2,384,1024]{1,2,0:T(8,128)(2,1)S(1)} collective-permute-done((bf16[2,384,1024]{1,2,0:T(8,128)(2,1)}, bf16[2,384,1024]{1,2,0:T(8,128)(2,1)S(1)}, u32[]{:S(2)}, u32[]{:S(2)}) %collective-permute-start) | collective-permute-done | bytes 1572896 | tf_op jit(solution)/shard_map/while/body/eval_jaxpr/ppermute | solution.py:18
  257.8 10.7 %conditional.4 = ((f32[16,384]{1,0:T(8,128)}, f32[16,384]{1,0:T(8,128)S(1)}, f32[384,1024]{0,1:T(8,128)})) conditional(s32[]{:T(128)} %convert_element_type.105, (f32[16,384]{1,0:T(8,128)}, f32[16,384]{1,0:T(8,128)S(1)}, f32[384,1024]{0,1:T(8,128)}) %tuple.73, (pred[3,128,384]{2,1,0:T(8,128)(4,1)S(1)}, bf16[2,384,1024]{1,2,0:T(8,128)(2,1)S(1)}, ...), branch_computations={%region_9.9_spmd, %region_10.12_spmd} | conditional | flops 630736896 | bytes 38092832 | solution.py:74
  263.3 4.6 bitcast_add_fusion.1
  269.7 8.5 %collective-permute-start = (bf16[2,384,1024]{1,2,0:T(8,128)(2,1)}, bf16[2,384,1024]{1,2,0:T(8,128)(2,1)S(1)}, u32[]{:S(2)}, u32[]{:S(2)}) collective-permute-start(bf16[2,384,1024]{1,2,0:T(8,128)(2,1)} %get-tuple-element.409), channel_id=1, source_target_pairs={{7,0},{0,1},{1,2},{2,3},{3,4},{4,5},{5,6},{6,7},{15,8},{8,9},{9,10... | collective-permute-start | bytes 4718600 | tf_op jit(solution)/shard_map/while/body/eval_jaxpr/ppermute | solution.py:18
  279.9 86.9 %collective-permute-done = bf16[2,384,1024]{1,2,0:T(8,128)(2,1)S(1)} collective-permute-done((bf16[2,384,1024]{1,2,0:T(8,128)(2,1)}, bf16[2,384,1024]{1,2,0:T(8,128)(2,1)S(1)}, u32[]{:S(2)}, u32[]{:S(2)}) %collective-permute-start) | collective-permute-done | bytes 1572896 | tf_op jit(solution)/shard_map/while/body/eval_jaxpr/ppermute | solution.py:18
  368.1 19.1 %collective-permute-start = (bf16[2,384,1024]{1,2,0:T(8,128)(2,1)}, bf16[2,384,1024]{1,2,0:T(8,128)(2,1)S(1)}, u32[]{:S(2)}, u32[]{:S(2)}) collective-permute-start(bf16[2,384,1024]{1,2,0:T(8,128)(2,1)} %get-tuple-element.409), channel_id=1, source_target_pairs={{7,0},{0,1},{1,2},{2,3},{3,4},{4,5},{5,6},{6,7},{15,8},{8,9},{9,10... | collective-permute-start | bytes 4718600 | tf_op jit(solution)/shard_map/while/body/eval_jaxpr/ppermute | solution.py:18
  388.9 84.1 %collective-permute-done = bf16[2,384,1024]{1,2,0:T(8,128)(2,1)S(1)} collective-permute-done((bf16[2,384,1024]{1,2,0:T(8,128)(2,1)}, bf16[2,384,1024]{1,2,0:T(8,128)(2,1)S(1)}, u32[]{:S(2)}, u32[]{:S(2)}) %collective-permute-start) | collective-permute-done | bytes 1572896 | tf_op jit(solution)/shard_map/while/body/eval_jaxpr/ppermute | solution.py:18
  474.2 8.4 %collective-permute-start = (bf16[2,384,1024]{1,2,0:T(8,128)(2,1)}, bf16[2,384,1024]{1,2,0:T(8,128)(2,1)S(1)}, u32[]{:S(2)}, u32[]{:S(2)}) collective-permute-start(bf16[2,384,1024]{1,2,0:T(8,128)(2,1)} %get-tuple-element.409), channel_id=1, source_target_pairs={{7,0},{0,1},{1,2},{2,3},{3,4},{4,5},{5,6},{6,7},{15,8},{8,9},{9,10... | collective-permute-start | bytes 4718600 | tf_op jit(solution)/shard_map/while/body/eval_jaxpr/ppermute | solution.py:18
  484.4 65.7 %collective-permute-done = bf16[2,384,1024]{1,2,0:T(8,128)(2,1)S(1)} collective-permute-done((bf16[2,384,1024]{1,2,0:T(8,128)(2,1)}, bf16[2,384,1024]{1,2,0:T(8,128)(2,1)S(1)}, u32[]{:S(2)}, u32[]{:S(2)}) %collective-permute-start) | collective-permute-done | bytes 1572896 | tf_op jit(solution)/shard_map/while/body/eval_jaxpr/ppermute | solution.py:18
  550.1 10.7 %conditional.4 = ((f32[16,384]{1,0:T(8,128)}, f32[16,384]{1,0:T(8,128)S(1)}, f32[384,1024]{0,1:T(8,128)})) conditional(s32[]{:T(128)} %convert_element_type.105, (f32[16,384]{1,0:T(8,128)}, f32[16,384]{1,0:T(8,128)S(1)}, f32[384,1024]{0,1:T(8,128)}) %tuple.73, (pred[3,128,384]{2,1,0:T(8,128)(4,1)S(1)}, bf16[2,384,1024]{1,2,0:T(8,128)(2,1)S(1)}, ...), branch_computations={%region_9.9_spmd, %region_10.12_spmd} | conditional | flops 630736896 | bytes 38092832 | solution.py:74
  563.7 25.9 %collective-permute-done = bf16[2,384,1024]{1,2,0:T(8,128)(2,1)S(1)} collective-permute-done((bf16[2,384,1024]{1,2,0:T(8,128)(2,1)}, bf16[2,384,1024]{1,2,0:T(8,128)(2,1)S(1)}, u32[]{:S(2)}, u32[]{:S(2)}) %collective-permute-start) | collective-permute-done | bytes 1572896 | tf_op jit(solution)/shard_map/while/body/eval_jaxpr/ppermute | solution.py:18
  590.9 17.6 %collective-permute-start = (bf16[2,384,1024]{1,2,0:T(8,128)(2,1)}, bf16[2,384,1024]{1,2,0:T(8,128)(2,1)S(1)}, u32[]{:S(2)}, u32[]{:S(2)}) collective-permute-start(bf16[2,384,1024]{1,2,0:T(8,128)(2,1)} %get-tuple-element.409), channel_id=1, source_target_pairs={{7,0},{0,1},{1,2},{2,3},{3,4},{4,5},{5,6},{6,7},{15,8},{8,9},{9,10... | collective-permute-start | bytes 4718600 | tf_op jit(solution)/shard_map/while/body/eval_jaxpr/ppermute | solution.py:18
  610.1 33.4 %collective-permute-done = bf16[2,384,1024]{1,2,0:T(8,128)(2,1)S(1)} collective-permute-done((bf16[2,384,1024]{1,2,0:T(8,128)(2,1)}, bf16[2,384,1024]{1,2,0:T(8,128)(2,1)S(1)}, u32[]{:S(2)}, u32[]{:S(2)}) %collective-permute-start) | collective-permute-done | bytes 1572896 | tf_op jit(solution)/shard_map/while/body/eval_jaxpr/ppermute | solution.py:18
  643.6 10.7 %conditional.4 = ((f32[16,384]{1,0:T(8,128)}, f32[16,384]{1,0:T(8,128)S(1)}, f32[384,1024]{0,1:T(8,128)})) conditional(s32[]{:T(128)} %convert_element_type.105, (f32[16,384]{1,0:T(8,128)}, f32[16,384]{1,0:T(8,128)S(1)}, f32[384,1024]{0,1:T(8,128)}) %tuple.73, (pred[3,128,384]{2,1,0:T(8,128)(4,1)S(1)}, bf16[2,384,1024]{1,2,0:T(8,128)(2,1)S(1)}, ...), branch_computations={%region_9.9_spmd, %region_10.12_spmd} | conditional | flops 630736896 | bytes 38092832 | solution.py:74
  649.0 4.6 bitcast_add_fusion.1
  (104 shorter events, 74.6 us)
Async XLA Ops:
  7.2 70.8 %all-gather.3.cloned.1.call-start = ((), (), s32[]{:S(2)}) async-start(), calls=%async_computation | async-start | bytes 6488064 | tf_op jit(solution)/shard_map/all_gather | solution.py:84
  7.9 650.3 %all-gather.5.cloned.1.call-start = ((), (), s32[]{:S(2)}) async-start(), calls=%async_computation.1 | async-start | bytes 2162688 | tf_op jit(solution)/shard_map/all_gather | solution.py:116
  92.3 3.6 copy-start
  103.9 65.8 %collective-permute-start = (bf16[2,384,1024]{1,2,0:T(8,128)(2,1)}, bf16[2,384,1024]{1,2,0:T(8,128)(2,1)S(1)}, u32[]{:S(2)}, u32[]{:S(2)}) collective-permute-start(bf16[2,384,1024]{1,2,0:T(8,128)(2,1)} %get-tuple-element.409), channel_id=1, source_target_pairs={{7,0},{0,1},{1,2},{2,3},{3,4},{4,5},{5,6},{6,7},{15,8},{8,9},{9,10... | collective-permute-start | bytes 4718600 | tf_op jit(solution)/shard_map/while/body/eval_jaxpr/ppermute | solution.py:18
  181.7 76.1 %collective-permute-start = (bf16[2,384,1024]{1,2,0:T(8,128)(2,1)}, bf16[2,384,1024]{1,2,0:T(8,128)(2,1)S(1)}, u32[]{:S(2)}, u32[]{:S(2)}) collective-permute-start(bf16[2,384,1024]{1,2,0:T(8,128)(2,1)} %get-tuple-element.409), channel_id=1, source_target_pairs={{7,0},{0,1},{1,2},{2,3},{3,4},{4,5},{5,6},{6,7},{15,8},{8,9},{9,10... | collective-permute-start | bytes 4718600 | tf_op jit(solution)/shard_map/while/body/eval_jaxpr/ppermute | solution.py:18
  269.7 97.1 %collective-permute-start = (bf16[2,384,1024]{1,2,0:T(8,128)(2,1)}, bf16[2,384,1024]{1,2,0:T(8,128)(2,1)S(1)}, u32[]{:S(2)}, u32[]{:S(2)}) collective-permute-start(bf16[2,384,1024]{1,2,0:T(8,128)(2,1)} %get-tuple-element.409), channel_id=1, source_target_pairs={{7,0},{0,1},{1,2},{2,3},{3,4},{4,5},{5,6},{6,7},{15,8},{8,9},{9,10... | collective-permute-start | bytes 4718600 | tf_op jit(solution)/shard_map/while/body/eval_jaxpr/ppermute | solution.py:18
  368.1 104.9 %collective-permute-start = (bf16[2,384,1024]{1,2,0:T(8,128)(2,1)}, bf16[2,384,1024]{1,2,0:T(8,128)(2,1)S(1)}, u32[]{:S(2)}, u32[]{:S(2)}) collective-permute-start(bf16[2,384,1024]{1,2,0:T(8,128)(2,1)} %get-tuple-element.409), channel_id=1, source_target_pairs={{7,0},{0,1},{1,2},{2,3},{3,4},{4,5},{5,6},{6,7},{15,8},{8,9},{9,10... | collective-permute-start | bytes 4718600 | tf_op jit(solution)/shard_map/while/body/eval_jaxpr/ppermute | solution.py:18
  474.2 75.9 %collective-permute-start = (bf16[2,384,1024]{1,2,0:T(8,128)(2,1)}, bf16[2,384,1024]{1,2,0:T(8,128)(2,1)S(1)}, u32[]{:S(2)}, u32[]{:S(2)}) collective-permute-start(bf16[2,384,1024]{1,2,0:T(8,128)(2,1)} %get-tuple-element.409), channel_id=1, source_target_pairs={{7,0},{0,1},{1,2},{2,3},{3,4},{4,5},{5,6},{6,7},{15,8},{8,9},{9,10... | collective-permute-start | bytes 4718600 | tf_op jit(solution)/shard_map/while/body/eval_jaxpr/ppermute | solution.py:18
  562.0 27.6 %collective-permute-start = (bf16[2,384,1024]{1,2,0:T(8,128)(2,1)}, bf16[2,384,1024]{1,2,0:T(8,128)(2,1)S(1)}, u32[]{:S(2)}, u32[]{:S(2)}) collective-permute-start(bf16[2,384,1024]{1,2,0:T(8,128)(2,1)} %get-tuple-element.409), channel_id=1, source_target_pairs={{7,0},{0,1},{1,2},{2,3},{3,4},{4,5},{5,6},{6,7},{15,8},{8,9},{9,10... | collective-permute-start | bytes 4718600 | tf_op jit(solution)/shard_map/while/body/eval_jaxpr/ppermute | solution.py:18
  590.9 52.6 %collective-permute-start = (bf16[2,384,1024]{1,2,0:T(8,128)(2,1)}, bf16[2,384,1024]{1,2,0:T(8,128)(2,1)S(1)}, u32[]{:S(2)}, u32[]{:S(2)}) collective-permute-start(bf16[2,384,1024]{1,2,0:T(8,128)(2,1)} %get-tuple-element.409), channel_id=1, source_target_pairs={{7,0},{0,1},{1,2},{2,3},{3,4},{4,5},{5,6},{6,7},{15,8},{8,9},{9,10... | collective-permute-start | bytes 4718600 | tf_op jit(solution)/shard_map/while/body/eval_jaxpr/ppermute | solution.py:18
  655.5 2.8 copy-start.1
  655.5 2.8 copy-start.2
Sparse Core Ops, SparseCore 0:
  9.9 68.1 all-gather.2
  79.9 126.7 all-gather.4
where the time goes:
time: 681 us; the launch traced here: 669 us
  waiting for transfers between devices  480 us (70%)
  starting transfers between devices  73.7 us (11%)
  matrix products  44.2 us (6%)
  other arithmetic  30.8 us (5%)
  local copies, waits for them, and re-layouts  20.1 us (3%)
  between operations  14.7 us (2%)
    ppermute x7, waiting for transfers between devices, from_behind(): return lax.ppermute(block, axis, route)  415 us
    ppermute x7, starting transfers between devices, from_behind(): return lax.ppermute(block, axis, route)  73.6 us
    all_gather x1, waiting for transfers between devices, on_device(): lax.all_gather(w_qkv, 'dp', axis=0, tiled=True)  64.2 us
    dot_general x5, matrix products, update(): jnp.einsum('hqk,khd->qhd', weights.astype(jnp.bfloat16), value_heads, pre...  25.3 us
  transfers between devices with their start and end apart: 9, of which 8 were waited for; matrix products, arithmetic and copies ran while one was open for 14% of the time, Pallas kernels for 0%

commit v1 on v0

v1 whole, which is shorter than its diff:
```python
import jax
import jax.numpy as jnp
from jax import lax
from jax.experimental import pallas as pl
from jax.experimental.pallas import tpu as pltpu
from jax.sharding import PartitionSpec as P

D = 1024
HEADS = 16
BLOCK = 128
NB = 24
STRIP = 384
STRIPS = 8
ROWS = 32
PAIRS = 8
CHUNKS = 4
CROWS = STRIP // CHUNKS
COLS = 512

NEG_FILL = -1e30
EPSILON = 1e-06
MESH = pl.DeviceIdType.MESH

SELF, BEFORE, AFTER, ACROSS = range(4)


def gather_kernel(tok_ref, gain_ref, beta_ref, wq_ref, bq_ref, wo_ref,
                  q_ref, k_hbm, v_hbm, wo_out,
                  toks, w_all, staged,
                  tsend, trecv, wsend, wrecv, ksem, vsem):
    dp = lax.axis_index("dp")
    sq = lax.axis_index("seq")
    core = lax.rem(dp, 2)
    x = lax.rem(dp // 2, 4)
    zl = dp // 8
    y = lax.rem(sq, 4)
    zh = sq // 4
    z = zh * 4 + zl

    def device(dx=0, dy=0, dz=0, flip=False):
        zz = lax.rem(z + dz + 8, 8)
        cc = 1 - core if flip else core
        return (lax.rem(zz, 4) * 8 + lax.rem(x + dx + 4, 4) * 2 + cc,
                (zz // 4) * 4 + lax.rem(y + dy + 4, 4))

    partners = [device(dx=1), device(dx=-1), device(dy=1), device(dy=-1), device(dz=1), device(dz=-1),
                device(dz=2), device(dz=-2), device(dz=4), device(flip=True)]
    barrier = pltpu.get_barrier_semaphore()
    for partner in partners:
        pl.semaphore_signal(barrier, inc=1, device_id=partner, device_id_type=MESH)
    pl.semaphore_wait(barrier, len(partners))

    def token_copy(plane, place, chunk):
        slot = plane * 4 + place
        if place == SELF:
            source, target = SELF, device(dz=4)
        elif place == BEFORE:
            source, target = plane * 4 + SELF, device(dy=1)
        elif place == AFTER:
            source, target = plane * 4 + SELF, device(dy=-1)
        elif chunk < CHUNKS // 2:
            source, target = plane * 4 + BEFORE, device(dy=1)
        else:
            source, target = plane * 4 + AFTER, device(dy=-1)
        rows = pl.ds(chunk * CROWS, CROWS)
        return pltpu.make_async_remote_copy(
            src_ref=toks.at[slot if False else source, rows], dst_ref=toks.at[slot, rows],
            send_sem=tsend.at[slot, chunk], recv_sem=trecv.at[slot, chunk],
            device_id=target, device_id_type=MESH)

    weights = (w_all, wo_out)

    def shard(k, dx, flip=False):
        zz = lax.rem(zl + (0, 3, 1, 2)[k], 4)
        cc = 1 - core if flip else core
        return zz * 8 + lax.rem(x + dx + 4, 4) * 2 + cc

    def weight_copy(which, name, k=0, place=SELF):
        ref = weights[which]
        first, count = 0, ROWS
        if name == "z":
            owner, index = shard(0, 0), k
            target = device(dz=(0, 1, -1, 2, -2)[k])
            if k >= 3:
                first, count = (k - 3) * (ROWS // 2), ROWS // 2
        elif name == "x":
            index = 5 + k * 4 + place
            if place == BEFORE:
                owner, target = shard(k, 0), device(dx=1)
            elif place == AFTER:
                owner, target = shard(k, 0), device(dx=-1)
            elif place == SELF:
                owner, target = shard(k, -1), device(dx=1)
                count = ROWS // 2
            else:
                owner, target = shard(k, 1), device(dx=-1)
                first, count = ROWS // 2, ROWS // 2
        else:
            index = 21 + k * 4 + place
            owner, target = shard(k, (0, -1, 1, 2)[place]), device(flip=True)
        rows = pl.ds(pl.multiple_of(owner * ROWS + first, ROWS // 2), count)
        return pltpu.make_async_remote_copy(
            src_ref=ref.at[rows], dst_ref=ref.at[rows],
            send_sem=wsend.at[which, index], recv_sem=wrecv.at[which, index],
            device_id=target, device_id_type=MESH)

    own_rows = pl.ds(pl.multiple_of(dp * ROWS, ROWS), ROWS)
    sent = []

    def go(copy):
        copy.start()
        sent.append(copy)

    w_all[own_rows, :] = wq_ref[...]
    wo_out[own_rows, :] = wo_ref[...]

    def spread(which, k):
        go(weight_copy(which, "x", k, BEFORE))
        go(weight_copy(which, "x", k, AFTER))
        go(weight_copy(which, "c", k, SELF))

    def around(which):
        for k in (1, 2, 3, 4):
            go(weight_copy(which, "z", k))
        spread(which, 0)

    def z_arrived(which, k):
        weight_copy(which, "z", k).wait_recv()
        if k == 3:
            weight_copy(which, "z", 4).wait_recv()
        spread(which, k)

    def x_arrived(which, k):
        weight_copy(which, "x", k, BEFORE).wait_recv()
        go(weight_copy(which, "x", k, SELF))
        go(weight_copy(which, "c", k, BEFORE))
        weight_copy(which, "x", k, AFTER).wait_recv()
        go(weight_copy(which, "x", k, ACROSS))
        go(weight_copy(which, "c", k, AFTER))

    def x_across(which, k):
        weight_copy(which, "x", k, SELF).wait_recv()
        weight_copy(which, "x", k, ACROSS).wait_recv()
        go(weight_copy(which, "c", k, ACROSS))

    def core_arrived(which):
        for k in range(4):
            for place in range(4):
                weight_copy(which, "c", k, place).wait_recv()

    def normalize(chunk):
        rows = pl.ds(chunk * CROWS, CROWS)
        values = tok_ref[rows, :].astype(jnp.float32)
        center = jnp.mean(values, axis=-1, keepdims=True)
        moved = values - center
        spread_ = jnp.mean(jnp.square(moved), axis=-1, keepdims=True)
        normed = moved * lax.rsqrt(spread_ + EPSILON)
        toks[SELF, rows, :] = (normed * gain_ref[...] + beta_ref[...]).astype(jnp.bfloat16)

    def offer(plane, chunk):
        go(token_copy(plane, BEFORE, chunk))
        go(token_copy(plane, AFTER, chunk))

    def pass_on(plane, chunk):
        token_copy(plane, BEFORE if chunk < CHUNKS // 2 else AFTER, chunk).wait_recv()
        go(token_copy(plane, ACROSS, chunk))

    def crossed(chunk):
        token_copy(1, SELF, chunk).wait_recv()
        offer(1, chunk)

    def rest(plane):
        for chunk in range(CHUNKS):
            token_copy(plane, AFTER if chunk < CHUNKS // 2 else BEFORE, chunk).wait_recv()

    def across(plane, chunks):
        for chunk in chunks:
            token_copy(plane, ACROSS, chunk).wait_recv()

    written = []

    def project(slot, first=0, count=STRIP):
        rows = slice(first, first + count)

        def body(n, _):
            cols = pl.ds(pl.multiple_of(D + n * COLS, COLS), COLS)
            made = jnp.dot(toks[slot, rows, :], w_all[:, cols], preferred_element_type=jnp.float32)
            staged[slot, rows, pl.ds(pl.multiple_of(n * COLS, COLS), COLS)] = (made + bq_ref[:, cols]).astype(jnp.bfloat16)
            return 0
        lax.fori_loop(0, 2 * D // COLS, body, 0)
        half = zh if slot < 4 else 1 - zh
        strip = half * 4 + lax.rem(y + (0, 3, 1, 2)[slot % 4], 4)
        there = pl.ds(pl.multiple_of(strip * STRIP + first, 64), count)
        part = 1 if first else 0
        for out, lane, sem in ((k_hbm, 0, ksem), (v_hbm, D, vsem)):
            copy = pltpu.make_async_copy(staged.at[slot, rows, lane:lane + D], out.at[there], sem.at[slot, part])
            copy.start()
            written.append(copy)

    around(0)
    for chunk in range(CHUNKS):
        normalize(chunk)
        offer(0, chunk)
        go(token_copy(1, SELF, chunk))
    z_arrived(0, 1)
    z_arrived(0, 2)
    pass_on(0, 0)
    x_arrived(0, 0)
    z_arrived(0, 3)
    pass_on(0, 1)
    crossed(0)
    x_arrived(0, 1)
    pass_on(0, 2)
    x_across(0, 0)
    x_arrived(0, 2)
    pass_on(0, 3)
    crossed(1)
    x_across(0, 1)
    x_arrived(0, 3)
    around(1)
    x_across(0, 2)
    x_across(0, 3)
    crossed(2)
    core_arrived(0)
    z_arrived(1, 1)
    z_arrived(1, 2)
    z_arrived(1, 3)

    def q_body(n, _):
        cols = pl.ds(pl.multiple_of(n * COLS, COLS), COLS)
        made = jnp.dot(toks[SELF], w_all[:, cols], preferred_element_type=jnp.float32)
        made = (made + bq_ref[:, cols]).astype(jnp.bfloat16)
        q_ref[:, cols] = made * jnp.bfloat16(0.125)
        return 0
    lax.fori_loop(0, D // COLS, q_body, 0)
    project(SELF)
    crossed(3)
    rest(0)
    pass_on(1, 0)
    pass_on(1, 1)
    project(BEFORE)
    x_arrived(1, 0)
    x_arrived(1, 1)
    project(AFTER)
    across(0, range(CHUNKS))
    x_arrived(1, 2)
    x_arrived(1, 3)
    pass_on(1, 2)
    project(ACROSS)
    pass_on(1, 3)
    project(4 + SELF)
    for k in range(4):
        x_across(1, k)
    rest(1)
    project(4 + BEFORE)
    project(4 + AFTER)
    half = CHUNKS // 2
    across(1, range(half))
    project(4 + ACROSS, 0, STRIP // 2)
    across(1, range(half, CHUNKS))
    project(4 + ACROSS, STRIP // 2, STRIP // 2)
    core_arrived(1)
    for copy in written:
        copy.wait()
    for copy in sent:
        copy.wait_send()


def gather(tokens, gain, beta, w_qkv, qkv_bias, w_out):
    vmem = pl.BlockSpec(memory_space=pltpu.VMEM)
    hbm = pl.BlockSpec(memory_space=pl.ANY)
    return pl.pallas_call(
        gather_kernel,
        name="gather_and_project",
        out_shape=(
            jax.ShapeDtypeStruct((STRIP, D), jnp.bfloat16),
            jax.ShapeDtypeStruct((STRIPS * STRIP, D), jnp.bfloat16),
            jax.ShapeDtypeStruct((STRIPS * STRIP, D), jnp.bfloat16),
            jax.ShapeDtypeStruct((D, D), jnp.bfloat16),
        ),
        in_specs=[vmem] * 6,
        out_specs=(vmem, hbm, hbm, vmem),
        scratch_shapes=[
            pltpu.VMEM((STRIPS, STRIP, D), jnp.bfloat16),
            pltpu.VMEM((D, 3 * D), jnp.bfloat16),
            pltpu.VMEM((STRIPS, STRIP, 2 * D), jnp.bfloat16),
            pltpu.SemaphoreType.DMA((STRIPS, CHUNKS)),
            pltpu.SemaphoreType.DMA((STRIPS, CHUNKS)),
            pltpu.SemaphoreType.DMA((2, 37)),
            pltpu.SemaphoreType.DMA((2, 37)),
            pltpu.SemaphoreType.DMA((STRIPS, 2)),
            pltpu.SemaphoreType.DMA((STRIPS, 2)),
        ],
        compiler_params=pltpu.CompilerParams(
            collective_id=0, has_side_effects=True, vmem_limit_bytes=44 * 2**20),
    )(tokens, gain, beta, w_qkv, qkv_bias, w_out)


def attend_kernel(m_ref, q_ref, k_hbm, v_hbm, tok_ref, wo_ref, bo_ref, upd_ref, ctx_ref,
                  idx, k_ref, v_ref, qz, s_scr, mx, lsum, acc, ksem, vsem):
    def fetch(hbm, ref, sem, j):
        rows = pl.ds(pl.multiple_of(j * BLOCK, BLOCK), BLOCK)
        return pltpu.make_async_copy(hbm.at[rows], ref.at[rows], sem.at[j])

    def each(hbm, ref, sem, start):
        def body(j, c):
            @pl.when(m_ref[0, j] + m_ref[1, j] + m_ref[2, j] > 0)
            def _():
                copy = fetch(hbm, ref, sem, j)
                if start:
                    copy.start()
                else:
                    copy.wait()
            return c
        lax.fori_loop(0, NB, body, 0)

    each(k_hbm, k_ref, ksem, True)
    each(v_hbm, v_ref, vsem, True)
    lane = lax.broadcasted_iota(jnp.int32, (BLOCK, 128), 1)
    low = lane < 64
    for i in range(STRIP // BLOCK):
        def build(j, c):
            idx[c] = j
            return c + (m_ref[i, j] > 0).astype(jnp.int32)
        n = lax.fori_loop(0, NB, build, jnp.int32(0))
        idx[n] = idx[n - 1]
        steps = (n + 1) // 2
        for hp in range(PAIRS):
            qv = q_ref[i * BLOCK:(i + 1) * BLOCK, hp * 128:(hp + 1) * 128]
            zero = jnp.zeros_like(qv)
            qz[hp, :BLOCK] = jnp.where(low, qv, zero)
            qz[hp, BLOCK:] = jnp.where(low, zero, qv)
        mx[...] = jnp.full_like(mx, NEG_FILL)
        lsum[...] = jnp.zeros_like(lsum)
        acc[...] = jnp.zeros_like(acc)
        if i == 0:
            each(k_hbm, k_ref, ksem, False)

        def pass1(t, _):
            r0 = pl.multiple_of(idx[2 * t] * BLOCK, BLOCK)
            r1 = pl.multiple_of(idx[2 * t + 1] * BLOCK, BLOCK)
            for hp in range(PAIRS):
                ln = slice(hp * 128, (hp + 1) * 128)
                kk = jnp.concatenate([k_ref[pl.ds(r0, BLOCK), ln], k_ref[pl.ds(r1, BLOCK), ln]], axis=0)
                s = lax.dot_general(qz[hp], kk, (((1,), (1,)), ((), ())), preferred_element_type=jnp.float32)
                s_scr[t, hp] = s
                mx[hp] = jnp.maximum(mx[hp], jnp.maximum(s[:, :128], s[:, 128:]))
            return 0
        lax.fori_loop(0, steps, pass1, 0)

        @pl.when(lax.rem(n, 2) == 1)
        def _():
            for hp in range(PAIRS):
                s_scr[steps - 1, hp, :, 128:] = jnp.full((256, 128), NEG_FILL, jnp.float32)
        for hp in range(PAIRS):
            mx[hp] = jnp.broadcast_to(jnp.max(mx[hp], axis=1, keepdims=True), (256, 128))
        if i == 0:
            each(v_hbm, v_ref, vsem, False)

        def pass2(t, _):
            r0 = pl.multiple_of(idx[2 * t] * BLOCK, BLOCK)
            r1 = pl.multiple_of(idx[2 * t + 1] * BLOCK, BLOCK)
            for hp in range(PAIRS):
                ln = slice(hp * 128, (hp + 1) * 128)
                s = s_scr[t, hp]
                mm = mx[hp]
                p0 = jnp.exp(s[:, :128] - mm)
                p1 = jnp.exp(s[:, 128:] - mm)
                lsum[hp] += p0 + p1
                pb = jnp.concatenate([p0.astype(jnp.bfloat16), p1.astype(jnp.bfloat16)], axis=1)
                vv = jnp.concatenate([v_ref[pl.ds(r0, BLOCK), ln], v_ref[pl.ds(r1, BLOCK), ln]], axis=0)
                acc[hp] += jnp.dot(pb, vv, preferred_element_type=jnp.float32)
            return 0
        lax.fori_loop(0, steps, pass2, 0)
        rows = slice(i * BLOCK, (i + 1) * BLOCK)
        for hp in range(PAIRS):
            o = acc[hp] / jnp.sum(lsum[hp], axis=1, keepdims=True)
            ctx_ref[rows, hp * 128:(hp + 1) * 128] = jnp.where(low, o[:BLOCK], o[BLOCK:]).astype(jnp.bfloat16)
        projected = jnp.dot(ctx_ref[rows], wo_ref[...], preferred_element_type=jnp.float32)
        upd_ref[rows] = (tok_ref[rows].astype(jnp.float32) + projected + bo_ref[...]).astype(jnp.bfloat16)


def attention(masks, q, k, v, tokens, w_out, out_bias):
    vmem = pl.BlockSpec(memory_space=pltpu.VMEM)
    hbm = pl.BlockSpec(memory_space=pl.ANY)
    return pl.pallas_call(
        attend_kernel,
        name="attend",
        out_shape=(jax.ShapeDtypeStruct((STRIP, D), jnp.bfloat16),) * 2,
        in_specs=[pl.BlockSpec(memory_space=pltpu.SMEM), vmem, hbm, hbm, vmem, vmem, vmem],
        out_specs=(vmem, vmem),
        scratch_shapes=[
            pltpu.SMEM((NB + 1,), jnp.int32),
            pltpu.VMEM((NB * BLOCK, D), jnp.bfloat16),
            pltpu.VMEM((NB * BLOCK, D), jnp.bfloat16),
            pltpu.VMEM((PAIRS, 256, 128), jnp.bfloat16),
            pltpu.VMEM((NB // 2, PAIRS, 256, 256), jnp.float32),
            pltpu.VMEM((PAIRS, 256, 128), jnp.float32),
            pltpu.VMEM((PAIRS, 256, 128), jnp.float32),
            pltpu.VMEM((PAIRS, 256, 128), jnp.float32),
            pltpu.SemaphoreType.DMA((NB,)),
            pltpu.SemaphoreType.DMA((NB,)),
        ],
        compiler_params=pltpu.CompilerParams(vmem_limit_bytes=58 * 2**20),
    )(masks, q, k, v, tokens, w_out, out_bias)


def on_device(tokens, masks, ln_gain, ln_bias, w_qkv, qkv_bias, w_out, out_bias):
    sheet = tokens[0]
    q, k, v, w_full = gather(sheet, ln_gain[None], ln_bias[None], w_qkv, qkv_bias[None], w_out)
    updated, context = attention(masks[0], q, k, v, sheet, w_full, out_bias[None])
    return (updated[None], context[None])


def solution(mesh):
    placed = (
        P("dp", "seq", None),
        P("dp", "seq", None),
        P(),
        P(),
        P("dp", None),
        P(),
        P("dp", None),
        P(),
    )
    return jax.shard_map(
        on_device,
        mesh=mesh,
        in_specs=placed,
        out_specs=(P("dp", "seq", None), P("dp", "seq", None)),
        check_vma=False,
    )
```

time: 681 us -> 115 us (0.17)
  the two profiles are of different devices: /device:TPU:28 before, /device:TPU:49 now
where the time goes in v1:
time: 115 us
  Pallas kernels  103 us (90%)
  local copies, waits for them, and re-layouts  11.1 us (10%)
    pallas_call x1, Pallas kernels, gather(): pl.pallas_call(gather_kernel, name='gather_and_project', out_shape=(jax.S...  78.6 us
    pallas_call x1, Pallas kernels, attention(): pl.pallas_call(attend_kernel, name='attend', out_shape=(jax.ShapeDtypeStr...  24.2 us
    unnamed x19, local copies, waits for them, and re-layouts  11.1 us

profile of v1, /device:TPU:49, one launch (start us, length us, event | category | flops | bytes accessed | tf_op | source)
XLA Modules:
  0.0 114.6 jit_solution(17193872315234437659)
XLA Ops:
  0.6 1.2 %copy.12 = s32[1,3,24]{2,1,0:T(4,128)} copy(s32[1,3,24]{2,0,1:T(1,128)} %param.9) | data formatting | bytes 576
  1.8 0.0 copy-start.1
  1.9 1.1 copy-done.1
  3.0 0.0 copy-start.4
  3.0 0.9 copy-done.4
  3.9 0.0 copy-start.5
  3.9 0.8 copy-done.5
  4.8 0.0 copy-start.6
  4.8 0.7 copy-done.6
  5.5 0.0 copy-start.7
  5.5 0.7 copy-done.7
  6.1 0.0 copy-start.8
  6.1 0.7 copy-done.8
  6.8 78.6 %gather_and_project.1 = (bf16[384,1024]{1,0:T(8,128)(2,1)S(1)}, bf16[3072,1024]{1,0:T(8,128)(2,1)S(1)}, bf16[3072,1024]{1,0:T(8,128)(2,1)}, bf16[1024,1024]{1,0:T(8,128)(2,1)S(1)}) custom-call(bf16[384,1024]{1,0:T(8,128)(2,1)S(1)} %bitcast.11, f32[1,1024]{1,0:T(1,128)S(1)} %bitcast.13, f32[1,1024]{1,0:T(1,128)S(1)} %bitcast.14, ...), custom_call_target="tpu_custom_call" | custom-call | tf_op jit(solution)/shard_map/gather_and_project/pallas_call | solution.py:272
  85.5 0.0 copy-start
  85.5 2.6 %copy-done = bf16[3072,1024]{1,0:T(8,128)(2,1)} copy-done((bf16[3072,1024]{1,0:T(8,128)(2,1)}, bf16[3072,1024]{1,0:T(8,128)(2,1)S(1)}, u32[]{:S(2)}) %copy-start) | copy-done | bytes 6291480
  88.1 0.0 copy-start.2
  88.1 1.3 %copy-done.2 = bf16[1024,1024]{1,0:T(8,128)(2,1)} copy-done((bf16[1024,1024]{1,0:T(8,128)(2,1)}, bf16[1024,1024]{1,0:T(8,128)(2,1)S(1)}, u32[]{:S(2)}) %copy-start.2) | copy-done | bytes 2097176
  89.5 0.0 copy-start.3
  89.5 0.9 copy-done.3
  90.4 24.2 %attend.1 = (bf16[384,1024]{1,0:T(8,128)(2,1)}, bf16[384,1024]{1,0:T(8,128)(2,1)}) custom-call(s32[3,24]{1,0:T(4,128)} %bitcast.15, bf16[384,1024]{1,0:T(8,128)(2,1)} %copy-done.3, bf16[3072,1024]{1,0:T(8,128)(2,1)} %copy-done, bf16[3072,1024]{1,0:T(8,128)(2,1)} %get-tuple-element.10.v_hbm, bf16[384,1024]{1,0:T(8,128)(2,1)} %bitcast.10, ...), custom_call_target="tpu_custom_call" | custom-call | tf_op jit(solution)/shard_map/attend/pallas_call | solution.py:386
Async XLA Ops:
  1.8 1.1 copy-start.1
  3.0 0.9 copy-start.4
  3.9 0.8 copy-start.5
  4.8 0.7 copy-start.6
  5.5 0.7 copy-start.7
  6.1 0.7 copy-start.8
  85.5 2.7 %copy-start = (bf16[3072,1024]{1,0:T(8,128)(2,1)}, bf16[3072,1024]{1,0:T(8,128)(2,1)S(1)}, u32[]{:S(2)}) copy-start(bf16[3072,1024]{1,0:T(8,128)(2,1)S(1)} %get-tuple-element.9.k_hbm) | copy-start | bytes 18874372
  88.1 1.3 %copy-start.2 = (bf16[1024,1024]{1,0:T(8,128)(2,1)}, bf16[1024,1024]{1,0:T(8,128)(2,1)S(1)}, u32[]{:S(2)}) copy-start(bf16[1024,1024]{1,0:T(8,128)(2,1)S(1)} %get-tuple-element.11.wo_ref) | copy-start | bytes 6291460
  89.5 0.9 copy-start.3

commit v2 on v1

v2 whole, which is shorter than its diff:
```python
import jax
import jax.numpy as jnp
from jax import lax
from jax.experimental import pallas as pl
from jax.experimental.pallas import tpu as pltpu
from jax.sharding import PartitionSpec as P

D = 1024
HEADS = 16
BLOCK = 128
NB = 24
STRIP = 384
STRIPS = 8
ROWS = 32
PAIRS = 8
CHUNKS = 8
AHEAD = 4
CROSSING = 2
CROWS = STRIP // CHUNKS

NEG_FILL = -1e30
EPSILON = 1e-06
MESH = pl.DeviceIdType.MESH

SELF, BEFORE, AFTER, ACROSS = range(4)


def gather_kernel(tok_hbm, gain_hbm, beta_hbm, wq_hbm, bq_hbm, wo_hbm,
                  q_hbm, k_hbm, v_hbm, wo_out,
                  tok_ref, gain_ref, beta_ref, bq_ref, toks, w_all, w_two, staged, q_ref,
                  tsend, trecv, wsend, wrecv, insem, ksem, vsem):
    dp = lax.axis_index("dp")
    sq = lax.axis_index("seq")
    core = lax.rem(dp, 2)
    x = lax.rem(dp // 2, 4)
    zl = dp // 8
    y = lax.rem(sq, 4)
    zh = sq // 4
    z = zh * 4 + zl

    def device(dx=0, dy=0, dz=0, flip=False):
        zz = lax.rem(z + dz + 8, 8)
        cc = 1 - core if flip else core
        return (lax.rem(zz, 4) * 8 + lax.rem(x + dx + 4, 4) * 2 + cc,
                (zz // 4) * 4 + lax.rem(y + dy + 4, 4))

    own_rows = pl.ds(pl.multiple_of(dp * ROWS, ROWS), ROWS)
    fills = [
        pltpu.make_async_copy(source, target, insem.at[i])
        for i, (source, target) in enumerate((
            (wq_hbm.at[:, D:], w_all.at[own_rows]), (tok_hbm, tok_ref), (wq_hbm.at[:, :D], w_two.at[own_rows, :D]),
            (wo_hbm, w_two.at[own_rows, D:]),
            (gain_hbm, gain_ref), (beta_hbm, beta_ref), (bq_hbm, bq_ref)))]
    for fill in fills:
        fill.start()

    partners = [device(dx=1), device(dx=-1), device(dy=1), device(dy=-1), device(dz=1), device(dz=-1),
                device(dz=2), device(dz=-2), device(dz=4), device(flip=True)]
    barrier = pltpu.get_barrier_semaphore()
    for partner in partners:
        pl.semaphore_signal(barrier, inc=1, device_id=partner, device_id_type=MESH)
    for fill in fills:
        fill.wait()
    pl.semaphore_wait(barrier, len(partners))

    def token_copy(plane, place, chunk):
        source = plane, SELF
        if place == SELF:
            source, target = (0, SELF), device(dz=4)
        elif place == BEFORE:
            target = device(dy=1)
        elif place == AFTER:
            target = device(dy=-1)
        elif chunk % 2 == 0:
            source, target = (plane, BEFORE), device(dy=1)
        else:
            source, target = (plane, AFTER), device(dy=-1)
        slot = plane * 4 + place
        return pltpu.make_async_remote_copy(
            src_ref=toks.at[source[0], chunk, source[1]], dst_ref=toks.at[plane, chunk, place],
            send_sem=tsend.at[slot, chunk], recv_sem=trecv.at[slot, chunk],
            device_id=target, device_id_type=MESH)

    weights = (w_all, w_two)

    def shard(k, dx):
        return lax.rem(zl + (0, 3, 1, 2)[k], 4) * 8 + lax.rem(x + dx + 4, 4) * 2 + core

    def weight_copy(which, name, k=0, place=SELF):
        ref = weights[which]
        first, count = 0, ROWS
        if name == "z":
            owner, index = shard(0, 0), k
            target = device(dz=(0, 1, -1, 2, -2)[k])
            if k >= 3:
                first, count = (k - 3) * (ROWS // 2), ROWS // 2
        elif name == "x":
            index = 5 + k * 4 + place
            if place == BEFORE:
                owner, target = shard(k, 0), device(dx=1)
            elif place == AFTER:
                owner, target = shard(k, 0), device(dx=-1)
            elif place == SELF:
                owner, target = shard(k, -1), device(dx=1)
                count = ROWS // 2
            else:
                owner, target = shard(k, 1), device(dx=-1)
                first, count = ROWS // 2, ROWS // 2
        else:
            index = 21 + k * 4 + place
            owner, target = shard(k, (0, -1, 1, 2)[place]), device(flip=True)
        rows = pl.ds(pl.multiple_of(owner * ROWS + first, ROWS // 2), count)
        return pltpu.make_async_remote_copy(
            src_ref=ref.at[rows], dst_ref=ref.at[rows],
            send_sem=wsend.at[which, index], recv_sem=wrecv.at[which, index],
            device_id=target, device_id_type=MESH)

    sent = []

    def go(copy):
        copy.start()
        sent.append(copy)

    def arrive(copy):
        copy.wait_recv()

    def spread(which, k):
        go(weight_copy(which, "x", k, BEFORE))
        go(weight_copy(which, "x", k, AFTER))
        go(weight_copy(which, "c", k, SELF))

    def around(which):
        for k in (1, 2, 3, 4):
            go(weight_copy(which, "z", k))

    def z_arrived(which, k):
        arrive(weight_copy(which, "z", k))
        if k == 3:
            arrive(weight_copy(which, "z", 4))
        spread(which, k)

    def x_arrived(which, k):
        arrive(weight_copy(which, "x", k, BEFORE))
        go(weight_copy(which, "x", k, SELF))
        go(weight_copy(which, "c", k, BEFORE))
        arrive(weight_copy(which, "x", k, AFTER))
        go(weight_copy(which, "x", k, ACROSS))
        go(weight_copy(which, "c", k, AFTER))

    def x_across(which, k):
        arrive(weight_copy(which, "x", k, SELF))
        arrive(weight_copy(which, "x", k, ACROSS))
        go(weight_copy(which, "c", k, ACROSS))

    def core_arrived(which):
        for k in range(4):
            for place in range(4):
                arrive(weight_copy(which, "c", k, place))

    def normalize(chunk):
        rows = pl.ds(chunk * CROWS, CROWS)
        values = tok_ref[rows, :].astype(jnp.float32)
        center = jnp.mean(values, axis=-1, keepdims=True)
        moved = values - center
        spread_ = jnp.mean(jnp.square(moved), axis=-1, keepdims=True)
        normed = moved * lax.rsqrt(spread_ + EPSILON)
        toks[0, chunk, SELF] = (normed * gain_ref[...] + beta_ref[...]).astype(jnp.bfloat16)

    def offer(plane, chunk):
        if chunk < CHUNKS:
            go(token_copy(plane, BEFORE, chunk))
            go(token_copy(plane, AFTER, chunk))

    def start():
        for chunk in range(CHUNKS):
            normalize(chunk)
            if chunk < AHEAD:
                offer(0, chunk)

    def cross(chunk):
        if chunk < CHUNKS:
            go(token_copy(1, SELF, chunk))

    def step(plane, chunk):
        first, second = (BEFORE, AFTER) if chunk % 2 == 0 else (AFTER, BEFORE)
        arrive(token_copy(plane, first, chunk))
        go(token_copy(plane, ACROSS, chunk))
        if plane == 0:
            offer(plane, chunk + AHEAD)
        arrive(token_copy(plane, second, chunk))

    def crossed(chunk):
        arrive(token_copy(1, SELF, chunk))
        cross(chunk + CROSSING)
        offer(1, chunk)

    def across(plane, chunks):
        for chunk in chunks:
            arrive(token_copy(plane, ACROSS, chunk))

    written = []

    def project(plane, first, end, piece):
        count = (end - first) * 4 * CROWS
        read = toks[plane, first:end].reshape(count, D)
        half = zh if plane == 0 else 1 - zh
        for lane, out, sem in ((0, k_hbm, ksem), (D, v_hbm, vsem)):
            made = jnp.dot(read, w_all[:, lane:D + lane], preferred_element_type=jnp.float32)
            made = (made + bq_ref[:, D + lane:2 * D + lane]).astype(jnp.bfloat16)
            staged[plane, first:end, :, :, lane:lane + D] = made.reshape(end - first, 4, CROWS, D)
            for place in range(4):
                strip = half * 4 + lax.rem(y + (0, 3, 1, 2)[place], 4)
                copy = pltpu.make_async_copy(
                    staged.at[plane, first:end, place, :, lane:lane + D], out.at[strip, first:end], sem.at[piece, place])
                copy.start()
                written.append(copy)

    def queries():
        own = toks[0, :, SELF].reshape(STRIP, D)
        made = jnp.dot(own, w_two[:, :D], preferred_element_type=jnp.float32)
        q_ref[...] = (made + bq_ref[:, :D]).astype(jnp.bfloat16) * jnp.bfloat16(0.125)
        copy = pltpu.make_async_copy(q_ref, q_hbm, insem.at[0])
        copy.start()
        written.append(copy)

    def output_weights():
        copy = pltpu.make_async_copy(w_two.at[:, D:], wo_out, insem.at[1])
        copy.start()
        written.append(copy)

    around(0)
    spread(0, 0)
    start()
    cross(0)
    step(0, 0)
    x_arrived(0, 0)
    step(0, 1)
    x_across(0, 0)
    z_arrived(0, 1)
    z_arrived(0, 2)
    z_arrived(0, 3)
    around(1)
    cross(1)
    step(0, 2)
    crossed(0)
    step(0, 3)
    step(0, 4)
    x_arrived(0, 1)
    x_arrived(0, 2)
    x_arrived(0, 3)
    spread(1, 0)
    step(0, 5)
    x_across(0, 1)
    x_across(0, 2)
    x_across(0, 3)
    z_arrived(1, 1)
    z_arrived(1, 2)
    z_arrived(1, 3)
    step(0, 6)
    crossed(1)
    core_arrived(0)
    x_arrived(1, 0)
    step(0, 7)
    across(0, range(CHUNKS))
    project(0, 0, 2, 0)
    crossed(2)
    step(1, 0)
    project(0, 2, 4, 1)
    x_arrived(1, 1)
    x_arrived(1, 2)
    x_arrived(1, 3)
    x_across(1, 0)
    crossed(3)
    step(1, 1)
    project(0, 4, 6, 2)
    crossed(4)
    step(1, 2)
    x_across(1, 1)
    x_across(1, 2)
    x_across(1, 3)
    project(0, 6, 8, 3)
    crossed(5)
    step(1, 3)
    across(1, (0, 1))
    project(1, 0, 2, 4)
    core_arrived(1)
    queries()
    crossed(6)
    step(1, 4)
    across(1, (2, 3))
    project(1, 2, 4, 5)
    crossed(7)
    step(1, 5)
    output_weights()
    step(1, 6)
    across(1, (4, 5))
    project(1, 4, 6, 6)
    step(1, 7)
    across(1, (6, 7))
    project(1, 6, 8, 7)
    for copy in written:
        copy.wait()
    for copy in sent:
        copy.wait_send()


def gather(tokens, gain, beta, w_qkv, qkv_bias, w_out):
    hbm = pl.BlockSpec(memory_space=pltpu.HBM)
    return pl.pallas_call(
        gather_kernel,
        name="gather_and_project",
        out_shape=(
            jax.ShapeDtypeStruct((STRIP, D), jnp.bfloat16),
            jax.ShapeDtypeStruct((STRIPS, CHUNKS, CROWS, D), jnp.bfloat16),
            jax.ShapeDtypeStruct((STRIPS, CHUNKS, CROWS, D), jnp.bfloat16),
            jax.ShapeDtypeStruct((D, D), jnp.bfloat16),
        ),
        in_specs=[hbm] * 6,
        out_specs=(hbm,) * 4,
        scratch_shapes=[
            pltpu.VMEM((STRIP, D), jnp.bfloat16),
            pltpu.VMEM((1, D), jnp.float32),
            pltpu.VMEM((1, D), jnp.float32),
            pltpu.VMEM((1, 3 * D), jnp.float32),
            pltpu.VMEM((2, CHUNKS, 4, CROWS, D), jnp.bfloat16),
            pltpu.VMEM((D, 2 * D), jnp.bfloat16),
            pltpu.VMEM((D, 2 * D), jnp.bfloat16),
            pltpu.VMEM((2, CHUNKS, 4, CROWS, 2 * D), jnp.bfloat16),
            pltpu.VMEM((STRIP, D), jnp.bfloat16),
            pltpu.SemaphoreType.DMA((STRIPS, CHUNKS)),
            pltpu.SemaphoreType.DMA((STRIPS, CHUNKS)),
            pltpu.SemaphoreType.DMA((2, 37)),
            pltpu.SemaphoreType.DMA((2, 37)),
            pltpu.SemaphoreType.DMA((7,)),
            pltpu.SemaphoreType.DMA((8, 4)),
            pltpu.SemaphoreType.DMA((8, 4)),
        ],
        compiler_params=pltpu.CompilerParams(
            collective_id=0, has_side_effects=True, vmem_limit_bytes=62 * 2**20),
    )(tokens, gain, beta, w_qkv, qkv_bias, w_out)


def attend_kernel(m_ref, q_hbm, k_hbm, v_hbm, tok_hbm, wo_hbm, bo_hbm, upd_ref, ctx_ref,
                  idx, k_ref, v_ref, qz, s_scr, mx, lsum, acc, q_ref, tok_ref, wo_ref, bo_ref, ksem, vsem, insem):
    def fetch(hbm, ref, sem, j):
        rows = pl.ds(pl.multiple_of(j * BLOCK, BLOCK), BLOCK)
        return pltpu.make_async_copy(hbm.at[rows], ref.at[rows], sem.at[j])

    def each(hbm, ref, sem, start):
        def body(j, c):
            @pl.when(m_ref[0, j] + m_ref[1, j] + m_ref[2, j] > 0)
            def _():
                copy = fetch(hbm, ref, sem, j)
                if start:
                    copy.start()
                else:
                    copy.wait()
            return c
        lax.fori_loop(0, NB, body, 0)

    fills = [pltpu.make_async_copy(source, target, insem.at[i]) for i, (source, target) in enumerate(
        ((q_hbm, q_ref), (wo_hbm, wo_ref), (tok_hbm, tok_ref), (bo_hbm, bo_ref)))]
    fills[0].start()
    each(k_hbm, k_ref, ksem, True)
    each(v_hbm, v_ref, vsem, True)
    for fill in fills[1:]:
        fill.start()
    fills[0].wait()
    lane = lax.broadcasted_iota(jnp.int32, (BLOCK, 128), 1)
    low = lane < 64
    for i in range(STRIP // BLOCK):
        def build(j, c):
            idx[c] = j
            return c + (m_ref[i, j] > 0).astype(jnp.int32)
        n = lax.fori_loop(0, NB, build, jnp.int32(0))
        idx[n] = idx[n - 1]
        steps = (n + 1) // 2
        for hp in range(PAIRS):
            qv = q_ref[i * BLOCK:(i + 1) * BLOCK, hp * 128:(hp + 1) * 128]
            zero = jnp.zeros_like(qv)
            qz[hp, :BLOCK] = jnp.where(low, qv, zero)
            qz[hp, BLOCK:] = jnp.where(low, zero, qv)
        mx[...] = jnp.full_like(mx, NEG_FILL)
        lsum[...] = jnp.zeros_like(lsum)
        acc[...] = jnp.zeros_like(acc)
        if i == 0:
            each(k_hbm, k_ref, ksem, False)

        def pass1(t, _):
            r0 = pl.multiple_of(idx[2 * t] * BLOCK, BLOCK)
            r1 = pl.multiple_of(idx[2 * t + 1] * BLOCK, BLOCK)
            for hp in range(PAIRS):
                ln = slice(hp * 128, (hp + 1) * 128)
                kk = jnp.concatenate([k_ref[pl.ds(r0, BLOCK), ln], k_ref[pl.ds(r1, BLOCK), ln]], axis=0)
                s = lax.dot_general(qz[hp], kk, (((1,), (1,)), ((), ())), preferred_element_type=jnp.float32)
                s_scr[t, hp] = s
                mx[hp] = jnp.maximum(mx[hp], jnp.maximum(s[:, :128], s[:, 128:]))
            return 0
        lax.fori_loop(0, steps, pass1, 0)

        @pl.when(lax.rem(n, 2) == 1)
        def _():
            for hp in range(PAIRS):
                s_scr[steps - 1, hp, :, 128:] = jnp.full((256, 128), NEG_FILL, jnp.float32)
        for hp in range(PAIRS):
            mx[hp] = jnp.broadcast_to(jnp.max(mx[hp], axis=1, keepdims=True), (256, 128))
        if i == 0:
            each(v_hbm, v_ref, vsem, False)

        def pass2(t, _):
            r0 = pl.multiple_of(idx[2 * t] * BLOCK, BLOCK)
            r1 = pl.multiple_of(idx[2 * t + 1] * BLOCK, BLOCK)
            for hp in range(PAIRS):
                ln = slice(hp * 128, (hp + 1) * 128)
                s = s_scr[t, hp]
                mm = mx[hp]
                p0 = jnp.exp(s[:, :128] - mm)
                p1 = jnp.exp(s[:, 128:] - mm)
                lsum[hp] += p0 + p1
                pb = jnp.concatenate([p0.astype(jnp.bfloat16), p1.astype(jnp.bfloat16)], axis=1)
                vv = jnp.concatenate([v_ref[pl.ds(r0, BLOCK), ln], v_ref[pl.ds(r1, BLOCK), ln]], axis=0)
                acc[hp] += jnp.dot(pb, vv, preferred_element_type=jnp.float32)
            return 0
        lax.fori_loop(0, steps, pass2, 0)
        rows = slice(i * BLOCK, (i + 1) * BLOCK)
        for hp in range(PAIRS):
            o = acc[hp] / jnp.sum(lsum[hp], axis=1, keepdims=True)
            ctx_ref[rows, hp * 128:(hp + 1) * 128] = jnp.where(low, o[:BLOCK], o[BLOCK:]).astype(jnp.bfloat16)
    for fill in fills[1:]:
        fill.wait()
    projected = jnp.dot(ctx_ref[...], wo_ref[...], preferred_element_type=jnp.float32)
    upd_ref[...] = (tok_ref[...].astype(jnp.float32) + projected + bo_ref[...]).astype(jnp.bfloat16)


def attention(masks, q, k, v, tokens, w_out, out_bias):
    vmem = pl.BlockSpec(memory_space=pltpu.VMEM)
    hbm = pl.BlockSpec(memory_space=pltpu.HBM)
    return pl.pallas_call(
        attend_kernel,
        name="attend",
        out_shape=(jax.ShapeDtypeStruct((STRIP, D), jnp.bfloat16),) * 2,
        in_specs=[pl.BlockSpec(memory_space=pltpu.SMEM)] + [hbm] * 6,
        out_specs=(vmem, vmem),
        scratch_shapes=[
            pltpu.SMEM((NB + 1,), jnp.int32),
            pltpu.VMEM((NB * BLOCK, D), jnp.bfloat16),
            pltpu.VMEM((NB * BLOCK, D), jnp.bfloat16),
            pltpu.VMEM((PAIRS, 256, 128), jnp.bfloat16),
            pltpu.VMEM((NB // 2, PAIRS, 256, 256), jnp.float32),
            pltpu.VMEM((PAIRS, 256, 128), jnp.float32),
            pltpu.VMEM((PAIRS, 256, 128), jnp.float32),
            pltpu.VMEM((PAIRS, 256, 128), jnp.float32),
            pltpu.VMEM((STRIP, D), jnp.bfloat16),
            pltpu.VMEM((STRIP, D), jnp.bfloat16),
            pltpu.VMEM((D, D), jnp.bfloat16),
            pltpu.VMEM((1, D), jnp.float32),
            pltpu.SemaphoreType.DMA((NB,)),
            pltpu.SemaphoreType.DMA((NB,)),
            pltpu.SemaphoreType.DMA((4,)),
        ],
        compiler_params=pltpu.CompilerParams(vmem_limit_bytes=62 * 2**20),
    )(masks, q, k, v, tokens, w_out, out_bias)


def on_device(tokens, masks, ln_gain, ln_bias, w_qkv, qkv_bias, w_out, out_bias):
    sheet = tokens[0]
    q, k, v, w_full = gather(sheet, ln_gain[None], ln_bias[None], w_qkv, qkv_bias[None], w_out)
    k, v = (array.reshape(STRIPS * STRIP, D) for array in (k, v))
    updated, context = attention(masks[0], q, k, v, sheet, w_full, out_bias[None])
    return (updated[None], context[None])


def solution(mesh):
    placed = (
        P("dp", "seq", None),
        P("dp", "seq", None),
        P(),
        P(),
        P("dp", None),
        P(),
        P("dp", None),
        P(),
    )
    return jax.shard_map(
        on_device,
        mesh=mesh,
        in_specs=placed,
        out_specs=(P("dp", "seq", None), P("dp", "seq", None)),
        check_vma=False,
    )
```

time: 115 us -> 105 us (0.913)
  the two profiles are of different devices: /device:TPU:49 before, /device:TPU:94 now
where the time goes in v2:
time: 105 us; the launch traced here: 104 us
  Pallas kernels  102 us (97%)
  local copies, waits for them, and re-layouts  1.26 us (1%)
    pallas_call x1, Pallas kernels, gather(): pl.pallas_call(gather_kernel, name='gather_and_project', out_shape=(jax.S...  78.6 us
    pallas_call x1, Pallas kernels, attention(): pl.pallas_call(attend_kernel, name='attend', out_shape=(jax.ShapeDtypeStr...  23.2 us

profile of v2, /device:TPU:94, one launch (start us, length us, event | category | flops | bytes accessed | tf_op | source)
XLA Modules:
  0.0 103.8 jit_solution(16855487324363892683)
XLA Ops:
  0.6 1.3 %copy.12 = s32[1,3,24]{2,1,0:T(4,128)} copy(s32[1,3,24]{2,0,1:T(1,128)} %param.9) | data formatting | bytes 576
  1.9 78.6 %gather_and_project.1 = (bf16[384,1024]{1,0:T(8,128)(2,1)}, bf16[8,8,48,1024]{3,2,1,0:T(8,128)(2,1)}, bf16[8,8,48,1024]{3,2,1,0:T(8,128)(2,1)}, bf16[1024,1024]{1,0:T(8,128)(2,1)}) custom-call(bf16[384,1024]{1,0:T(8,128)(2,1)} %bitcast.14, f32[1,1024]{1,0:T(1,128)} %bitcast.18, f32[1,1024]{1,0:T(1,128)} %bitcast.19, bf16[32,3072]{1,0:T(8,128)(2,1)} %wq_hbm.1, ...), custom_call_target="tpu_custom_call" | custom-call | tf_op jit(solution)/shard_map/gather_and_project/pallas_call | solution.py:309
  80.5 23.2 %attend.1 = (bf16[384,1024]{1,0:T(8,128)(2,1)}, bf16[384,1024]{1,0:T(8,128)(2,1)}) custom-call(s32[3,24]{1,0:T(4,128)} %bitcast.17, bf16[384,1024]{1,0:T(8,128)(2,1)} %get-tuple-element.8.q_hbm, bf16[3072,1024]{1,0:T(8,128)(2,1)} %bitcast.12, bf16[3072,1024]{1,0:T(8,128)(2,1)} %bitcast.13, bf16[384,1024]{1,0:T(8,128)(2,1)} %bitcast.15, ...), custom_call_target="tpu_custom_call" | custom-call | tf_op jit(solution)/shard_map/attend/pallas_call | solution.py:438

commit v3 on v2

--- a/solution.py
+++ b/solution.py
@@ -293,11 +293,11 @@
     step(1, 5)
     output_weights()
     step(1, 6)
-    across(1, (4, 5))
-    project(1, 4, 6, 6)
+    across(1, (4, 5, 6))
+    project(1, 4, 7, 6)
     step(1, 7)
-    across(1, (6, 7))
-    project(1, 6, 8, 7)
+    across(1, (7,))
+    project(1, 7, 8, 7)
     for copy in written:
         copy.wait()
     for copy in sent:

time: 105 us -> 104 us (level)
  the two profiles are of different devices: /device:TPU:94 before, /device:TPU:28 now
where the time goes in v3:
time: 104 us; the launch traced here: 105 us
  Pallas kernels  103 us (99%)
  local copies, waits for them, and re-layouts  1.26 us (1%)
    pallas_call x1, Pallas kernels, gather(): pl.pallas_call(gather_kernel, name='gather_and_project', out_shape=(jax.S...  78.7 us
    pallas_call x1, Pallas kernels, attention(): pl.pallas_call(attend_kernel, name='attend', out_shape=(jax.ShapeDtypeStr...  24 us

profile of v3, /device:TPU:28, one launch (start us, length us, event | category | flops | bytes accessed | tf_op | source)
XLA Modules:
  0.0 104.8 jit_solution(9007552552142324126)
XLA Ops:
  0.6 1.3 %copy.12 = s32[1,3,24]{2,1,0:T(4,128)} copy(s32[1,3,24]{2,0,1:T(1,128)} %param.9) | data formatting | bytes 576
  1.9 78.7 %gather_and_project.1 = (bf16[384,1024]{1,0:T(8,128)(2,1)}, bf16[8,8,48,1024]{3,2,1,0:T(8,128)(2,1)}, bf16[8,8,48,1024]{3,2,1,0:T(8,128)(2,1)}, bf16[1024,1024]{1,0:T(8,128)(2,1)}) custom-call(bf16[384,1024]{1,0:T(8,128)(2,1)} %bitcast.14, f32[1,1024]{1,0:T(1,128)} %bitcast.18, f32[1,1024]{1,0:T(1,128)} %bitcast.19, bf16[32,3072]{1,0:T(8,128)(2,1)} %wq_hbm.1, ...), custom_call_target="tpu_custom_call" | custom-call | tf_op jit(solution)/shard_map/gather_and_project/pallas_call | solution.py:309
  80.6 24.0 %attend.1 = (bf16[384,1024]{1,0:T(8,128)(2,1)}, bf16[384,1024]{1,0:T(8,128)(2,1)}) custom-call(s32[3,24]{1,0:T(4,128)} %bitcast.17, bf16[384,1024]{1,0:T(8,128)(2,1)} %get-tuple-element.8.q_hbm, bf16[3072,1024]{1,0:T(8,128)(2,1)} %bitcast.12, bf16[3072,1024]{1,0:T(8,128)(2,1)} %bitcast.13, bf16[384,1024]{1,0:T(8,128)(2,1)} %bitcast.15, ...), custom_call_target="tpu_custom_call" | custom-call | tf_op jit(solution)/shard_map/attend/pallas_call | solution.py:438
